TPU v7x, 512 devices: a whole 4x8x8 slice. The times are simulated.
512 devices in a mesh: pipe: 8 (over y_lo, x), expert: 64 (over y_hi, z, core).
Axes of the slice: x: 4, y: 8 (y_hi: 4, y_lo: 2; y = y_hi * 2 + y_lo), z: 8, core: 2. Of those that a mesh axis runs over, the one named last changes fastest.
Arguments:
- state: bfloat16 [64, 8, 128, 2048], P('expert', 'pipe'), may hold values from -24 to 24
- query: bfloat16 [64, 8, 128, 2048], P('expert', 'pipe'), may hold values from -8 to 8
- enc_kv: bfloat16 [64, 256, 2, 2048], P('expert', 'pipe'), may hold values from -4 to 4
- gain: float32 [2048], replicated, may hold values from 0.1 to 1.9
- w_in: bfloat16 [2048, 24576], P(None, 'expert'), may hold values from -0.125 to 0.125
- w_out: bfloat16 [24576, 2048], P('expert'), may hold values from -0.109375 to 0.109375
- expert_id: int32 [64, 8, 128], P('expert', 'pipe'), may hold values from 0 to 7
- slot: int32 [64, 8, 128], P('expert', 'pipe'), may hold values from -1 to 23, as said below
- gate: float32 [64, 8, 128], P('expert', 'pipe'), may hold values from 0.3 to 1
Outputs:
- output: bfloat16 [64, 8, 128, 2048], P('expert', 'pipe')
Inputs may be any that keep to these rules, and one draw needn't show every extreme that they name: Within the 128 tokens of one source and sample, the tokens sent to one expert take slots 0, 1, 2, ... in token order until 24 are taken; later ones have slot -1. In every draw some expert is given 24 slotted tokens by every source and sample.
All inputs are finite; a program needn't handle non-finite values.
Results may differ from a plain program's by a relative error of at most 0.0055.
Values may be sent and summed in bfloat16 or wider, within the bound.
A program may use at most 128 MiB of HBM per device.

v0:
```python
import math

import jax
import jax.numpy as jnp
from jax import lax
from jax.sharding import PartitionSpec as P

HEADS = 16
HD = 128
WSPLIT = 8


def expert_ffn(slot_rows, w_in, w_out):
    senders, slots_here, width = slot_rows.shape
    flat_rows = slot_rows.reshape(senders * slots_here, width)
    activation = jnp.maximum(
        jnp.dot(flat_rows, w_in, preferred_element_type=jnp.float32), 0.0
    ).astype(jnp.bfloat16)
    partial_value = jnp.dot(activation, w_out, preferred_element_type=jnp.float32).astype(
        jnp.bfloat16
    )
    return partial_value.reshape(senders, slots_here, width)


def body(state, query, enc_kv, gain, w_in, w_out, expert_id, slot, gate):
    tokens = state.shape[2]
    width = state.shape[3]
    queries = query.reshape(tokens, HEADS, HD)
    scale = 1.0 / math.sqrt(HD)
    kv_piece = lax.all_gather(enc_kv, "pipe", axis=1, tiled=True)
    best_score = jnp.full((HEADS, tokens), -jnp.inf, jnp.float32)
    denominator = jnp.zeros((HEADS, tokens), jnp.float32)
    accumulated = jnp.zeros((HEADS, tokens, HD), jnp.float32)
    key_rows = kv_piece[0, :, 0].reshape(-1, HEADS, HD)
    value_rows = kv_piece[0, :, 1].reshape(-1, HEADS, HD)
    scores = (
        jnp.einsum("thd,lhd->htl", queries, key_rows, preferred_element_type=jnp.float32) * scale
    )
    new_best = jnp.max(scores, axis=2)
    factor = jnp.exp(best_score - new_best)
    raised = jnp.exp(scores - new_best[:, :, None])
    denominator = denominator * factor + jnp.sum(raised, axis=2)
    update = jnp.einsum(
        "htl,lhd->htd", raised.astype(jnp.bfloat16), value_rows, preferred_element_type=jnp.float32
    )
    best_score, denominator, accumulated = (
        new_best,
        denominator,
        accumulated * factor[:, :, None] + update,
    )
    attended = jnp.transpose(accumulated / denominator[:, :, None], (1, 0, 2)).reshape(
        tokens, width
    )
    hidden_state = state[0, 0].astype(jnp.float32) + attended
    mean_square = jnp.mean(hidden_state * hidden_state, axis=-1, keepdims=True)
    normed = (hidden_state * lax.rsqrt(mean_square + 1e-06) * gain).astype(jnp.bfloat16)
    experts = lax.axis_size("expert") // WSPLIT
    capacity = 3 * tokens // (2 * experts)
    flat_slot = jnp.where(slot[0, 0] >= 0, expert_id[0, 0] * capacity + slot[0, 0], -1)
    slot_ids = jnp.arange(experts * capacity, dtype=jnp.int32)
    selector = (slot_ids[:, None] == flat_slot[None, :]).astype(jnp.bfloat16)
    packed = jnp.dot(selector, normed, preferred_element_type=jnp.float32).astype(jnp.bfloat16)
    copies = jnp.broadcast_to(
        packed.reshape(experts, 1, capacity, width), (experts, WSPLIT, capacity, width)
    )
    copies = copies.reshape(experts * WSPLIT, capacity, width)
    partial_value = expert_ffn(
        lax.all_to_all(copies, "expert", split_axis=0, concat_axis=0, tiled=True), w_in, w_out
    )
    returned = lax.all_to_all(partial_value, "expert", split_axis=0, concat_axis=0, tiled=True)
    summed = jnp.sum(returned.reshape(experts, WSPLIT, capacity, width), axis=1, dtype=jnp.float32)
    summed = summed.reshape(experts * capacity, width)
    picked = jnp.take(summed, jnp.maximum(flat_slot, 0), axis=0)
    contribution = jnp.where((flat_slot >= 0)[:, None], gate[0, 0][:, None] * picked, 0.0)
    output = (hidden_state + contribution).astype(jnp.bfloat16)
    return output.reshape(1, 1, tokens, width)


def solution(mesh):
    return jax.shard_map(
        body,
        mesh=mesh,
        in_specs=(
            P("expert", "pipe", None, None),
            P("expert", "pipe", None, None),
            P("expert", "pipe", None, None),
            P(),
            P(None, "expert"),
            P("expert", None),
            P("expert", "pipe", None),
            P("expert", "pipe", None),
            P("expert", "pipe", None),
        ),
        out_specs=P("expert", "pipe", None, None),
        check_vma=False,
    )
```

profile of v0, /device:TPU:288, one launch (start us, length us, event | category | flops | bytes accessed | tf_op | source)
XLA Modules:
  0.0 509.5 jit_solution(5332171025868441447)
XLA Ops:
  6.5 0.0 copy-start
  6.5 0.0 copy-start.6
  6.5 0.0 copy-start.5
  6.5 0.0 all-gather.2.cloned.1.call-start
  6.5 0.7 all-gather.2.cloned.1.call-update
  7.3 1.1 copy.31
  8.4 2.2 copy.28
  10.7 0.0 copy-done.6
  10.7 0.0 copy-done.5
  10.7 46.0 %all-gather.2.cloned.1.call-done = bf16[1,256,2,2048]{3,2,0,1:T(2,128)(2,1)} async-done(((bf16[1,32,2,2048]{3,2,0,1:T(2,128)(2,1)}), bf16[1,256,2,2048]{3,2,0,1:T(2,128)(2,1)}) %all-gather.2.cloned.1.call-update) | async-done | bytes 2097168 | tf_op jit(solution)/shard_map/all_gather | solution.py:30
  56.6 6.8 %fusion.24 = (bf16[1,256,1,2048]{3,2,0,1:T(2,128)(2,1)}, bf16[1,256,1,2048]{3,2,0,1:T(2,128)(2,1)}) fusion(bf16[1,256,2,2048]{3,2,0,1:T(2,128)(2,1)} %all-gather.2.cloned.1.call-done), kind=kLoop, calls=%fused_computation.42 | loop fusion | bytes 4194304 | tf_op jit(solution)/shard_map/slice | solution.py:34
  63.4 4.5 copy.30
  68.0 0.5 multiply_reduce_fusion
  68.5 0.0 copy-start.1
  68.5 1.3 copy-done.1
  69.8 0.8 fusion.1
  70.6 5.8 %copy.25 = bf16[1,256,1,2048]{1,3,2,0:T(8,128)(2,1)} copy(bf16[1,256,1,2048]{3,2,0,1:T(2,128)(2,1)} %get-tuple-element.8) | data formatting | bytes 2097152 | tf_op jit(solution)/shard_map/slice | solution.py:35
  76.4 2.8 multiply_reduce_fusion.1
  79.2 0.0 copy-start.2
  79.2 0.0 copy-start.3
  79.2 1.3 copy.27
  80.5 0.0 copy-done.2
  80.5 0.0 copy-done.3
  80.5 1.7 convolution_convert_fusion.1
  82.2 0.8 broadcast_in_dim.54
  83.0 173.5 %all_to_all.10 = bf16[64,24,2048]{2,1,0:T(8,128)(2,1)} all-to-all(bf16[64,24,2048]{2,1,0:T(8,128)(2,1)S(1)} %bitcast.61), channel_id=1, replica_groups=mesh['pipe'=8,'expert'=64] {'expert'}, dimensions={0} | all-to-all | bytes 12582912 | tf_op jit(solution)/shard_map/all_to_all | solution.py:68
  256.5 0.0 copy-done
  256.5 10.9 %convolution_convert_fusion = bf16[1536,2048]{1,0:T(8,128)(2,1)} fusion(bf16[384,2048]{1,0:T(8,128)(2,1)S(1)} %copy-done, bf16[1536,2048]{1,0:T(8,128)(2,1)} %bitcast.63, bf16[2048,384]{1,0:T(8,128)(2,1)} %param.13), kind=kOutput, calls=%fused_computation.2 | convolution fusion | flops 4836163584 | bytes 15728640 | tf_op jit(solution)/shard_map/dot_general | solution.py:19
  267.4 12.9 %all-to-all-start.1 = ((bf16[64,24,2048]{2,1,0:T(8,128)(2,1)}), bf16[64,24,2048]{2,1,0:T(8,128)(2,1)}, u32[]{:S(2)}, u32[]{:S(2)}) async-start(bf16[64,24,2048]{2,1,0:T(8,128)(2,1)} %bitcast.62), calls=%async_computation.1 | async-start | bytes 12582912 | tf_op jit(solution)/shard_map/all_to_all | solution.py:70
  280.3 1.4 copy.26
  281.7 212.0 %all-to-all-done.1 = bf16[64,24,2048]{2,1,0:T(8,128)(2,1)} async-done(((bf16[64,24,2048]{2,1,0:T(8,128)(2,1)}), bf16[64,24,2048]{2,1,0:T(8,128)(2,1)}, u32[]{:S(2)}, u32[]{:S(2)}) %all-to-all-start.1) | async-done | bytes 6291488 | tf_op jit(solution)/shard_map/all_to_all | solution.py:70
  493.7 4.1 convert_reduce_fusion
  497.9 0.0 copy-start.4
  497.9 1.9 gather_fusion
  499.8 0.0 copy-done.4
  499.8 2.9 fusion.9
  (7 shorter events, 0.0 us)
Async XLA Ops:
  6.5 250.0 %copy-start = (bf16[384,2048]{1,0:T(8,128)(2,1)S(1)}, bf16[384,2048]{1,0:T(8,128)(2,1)}, u32[]{:S(2)}) copy-start(bf16[384,2048]{1,0:T(8,128)(2,1)} %param.14) | copy-start | bytes 4718596
  6.5 4.1 copy-start.6
  6.5 4.1 copy-start.5
  6.5 50.1 %all-gather.2.cloned.1.call-start = ((), (), s32[]{:S(2)}) async-start(), calls=%async_computation.2 | async-start | bytes 2359296 | tf_op jit(solution)/shard_map/all_gather | solution.py:30
  68.5 1.3 copy-start.1
  79.2 1.3 copy-start.2
  79.2 1.3 copy-start.3
  267.4 226.3 %all-to-all-start.1 = ((bf16[64,24,2048]{2,1,0:T(8,128)(2,1)}), bf16[64,24,2048]{2,1,0:T(8,128)(2,1)}, u32[]{:S(2)}, u32[]{:S(2)}) async-start(bf16[64,24,2048]{2,1,0:T(8,128)(2,1)} %bitcast.62), calls=%async_computation.1 | async-start | bytes 12582912 | tf_op jit(solution)/shard_map/all_to_all | solution.py:70
  497.9 1.9 copy-start.4
Sparse Core Ops, SparseCore 0:
  9.4 47.1 all-gather.1
where the time goes:
time: 510 us
  waiting for transfers between devices  259 us (51%)
  blocking collectives  174 us (34%)
  local copies, waits for them, and re-layouts  27.2 us (5%)
  matrix products  15.9 us (3%)
  between operations  13.5 us (3%)
  starting transfers between devices  12.9 us (3%)
  other arithmetic  7.85 us (2%)
    all_to_all x1, waiting for transfers between devices, body(): lax.all_to_all(partial_value, 'expert', split_axis=0, concat_axis=0, tile...  212 us
    all_to_all x1, blocking collectives, body(): lax.all_to_all(copies, 'expert', split_axis=0, concat_axis=0, tiled=True)  174 us
    all_gather x1, waiting for transfers between devices, body(): kv_piece = lax.all_gather(enc_kv, 'pipe', axis=1, tiled=True)  46 us
    all_to_all x1, starting transfers between devices, body(): lax.all_to_all(partial_value, 'expert', split_axis=0, concat_axis=0, tile...  12.9 us
    dot_general x1, matrix products, expert_ffn(): jnp.dot(activation, w_out, preferred_element_type=jnp.float32)  10.9 us
  transfers between devices with their start and end apart: 2, of which 2 were waited for; matrix products, arithmetic and copies ran while one was open for 1% of the time, Pallas kernels for 0%

commit v1 on v0

v1 whole, which is shorter than its diff:
```python
import math

import jax
import jax.numpy as jnp
from jax import lax
from jax.experimental import pallas as pl
from jax.experimental.pallas import tpu as pltpu
from jax.sharding import PartitionSpec as P

HEADS = 16
HD = 128
D = 2048
TOK = 128
CAP = 24
POS = 32
ITEM = 4 * CAP
HALF = 2 * CAP
FF = 384
PASS = 8
FAR = 9
MESH = pl.DeviceIdType.MESH
F32 = jnp.float32
BF16 = jnp.bfloat16


def rows_at(start, count):
    return pl.ds(pl.multiple_of(start, 16), count)


def regroup(half, source_dim):
    at = lax.broadcasted_iota(jnp.int32, (2 * ITEM, 2 * ITEM), source_dim)
    other = lax.broadcasted_iota(jnp.int32, (2 * ITEM, 2 * ITEM), 1 - source_dim)
    far = (at >= ITEM).astype(jnp.int32)
    within = at - far * ITEM
    source = sum((within >= CAP * j).astype(jnp.int32) for j in (1, 2, 3))
    upper = far + half - 2 * far * half
    return jnp.where(other == within + source * CAP + upper * CAP, 1.0, 0.0).astype(BF16)


def kernel(
    state_ref, query_ref, kv_ref, gain_ref, srow_ref, scol_ref, gate_ref, win_ref, wout_ref,
    out_ref,
    kvb, hid, pk, y, x, r, c, res, w1, w2,
    kv_send, kv_recv, w_local, w_send, w_recv,
    y_send, y_recv, f_send, x_recv, x_send, r_send, c_recv, p_send, yr_send, res_recv,
):
    p = lax.axis_index("pipe")
    i = lax.axis_index("expert")
    px, py = lax.rem(p, 4), lax.div(p, 4)
    yh, z, core = lax.div(i, 16), lax.rem(lax.div(i, 2), 8), lax.rem(i, 2)
    half, k = lax.div(z, 4), lax.rem(z, 4)

    def pipe_dev(y, xx):
        return {"pipe": y * 4 + xx}

    def exp_dev(y, zz):
        return {"expert": (y * 8 + zz) * 2 + core}

    x_right, x_left = lax.rem(px + 1, 4), lax.rem(px + 3, 4)
    z_right, z_left = lax.rem(z + 1, 8), lax.rem(z + 7, 8)

    barrier = pltpu.get_barrier_semaphore()
    peers = [
        pipe_dev(1 - py, px), pipe_dev(py, x_right), pipe_dev(py, x_left),
        {"expert": i + 1 - 2 * core}, exp_dev(yh, z_right), exp_dev(yh, z_left),
    ] + [exp_dev(lax.rem(yh + j, 4), z) for j in (1, 2, 3)]
    for peer in peers:
        pl.semaphore_signal(barrier, inc=1, device_id=peer, device_id_type=MESH)
    pl.semaphore_wait(barrier, len(peers))

    def remote(src, dst, send, recv, device):
        return pltpu.make_async_remote_copy(
            src_ref=src, dst_ref=dst, send_sem=send, recv_sem=recv,
            device_id=device, device_id_type=MESH,
        )

    def kv_slot(owner):
        return pl.ds(pl.multiple_of(owner * POS, POS), POS)

    partner = (1 - py) * 4 + px
    kv_copies = []
    copy = remote(kv_ref, kvb.at[:, kv_slot(p), :], kv_send.at[0], kv_recv.at[0], pipe_dev(1 - py, px))
    copy.start()
    kv_copies.append(copy)
    for n, target in ((1, x_right), (2, x_left)):
        copy = remote(kv_ref, kvb.at[:, kv_slot(p), :], kv_send.at[n], kv_recv.at[n], pipe_dev(py, target))
        copy.start()
        kv_copies.append(copy)

    sibling = {"expert": i + 1 - 2 * core}
    w_copies = [
        remote(win_ref, w1.at[:, pl.ds(FF, FF)], w_send.at[0], w_recv.at[0], sibling),
        remote(wout_ref, w2.at[pl.ds(FF, FF), :], w_send.at[1], w_recv.at[1], sibling),
    ]
    w_locals = [
        pltpu.make_async_copy(win_ref, w1.at[:, pl.ds(0, FF)], w_local.at[0]),
        pltpu.make_async_copy(wout_ref, w2.at[pl.ds(0, FF), :], w_local.at[1]),
    ]
    for copy in w_locals + w_copies:
        copy.start()

    kvb[:, kv_slot(p), :] = kv_ref[...]
    kv_copies[0].wait_recv()
    for n, target in ((3, x_right), (4, x_left)):
        block = kvb.at[:, kv_slot(partner), :]
        copy = remote(block, block, kv_send.at[n], kv_recv.at[n], pipe_dev(py, target))
        copy.start()
        kv_copies.append(copy)
    far_copies = []
    for n, row in ((1, py), (3, 1 - py)):
        kv_copies[n].wait_recv()
        block = kvb.at[0, kv_slot(row * 4 + x_left), :]
        copy = remote(block, block, kv_send.at[4 + n], kv_recv.at[4 + n], pipe_dev(py, x_right))
        copy.start()
        far_copies.append(copy)
        kv_copies[n + 1].wait_recv()
        block = kvb.at[1, kv_slot(row * 4 + x_right), :]
        copy = remote(block, block, kv_send.at[5 + n], kv_recv.at[5 + n], pipe_dev(py, x_left))
        copy.start()
        far_copies.append(copy)
    for copy in far_copies:
        copy.wait_recv()

    scale = 1.0 / math.sqrt(HD)

    def head(h, squares):
        cols = pl.ds(pl.multiple_of(h * HD, HD), HD)
        scores = lax.dot_general(
            query_ref[:, cols], kvb[0, :, cols], (((1,), (1,)), ((), ())), preferred_element_type=F32
        ) * scale
        raised = jnp.exp(scores - jnp.max(scores, axis=1, keepdims=True))
        denominator = jnp.sum(raised, axis=1, keepdims=True)
        mixed = jnp.dot(raised.astype(BF16), kvb[1, :, cols], preferred_element_type=F32)
        hidden = state_ref[:, cols].astype(F32) + mixed / denominator
        hid[:, cols] = hidden
        return squares + hidden * hidden

    squares = lax.fori_loop(0, HEADS, head, jnp.zeros((TOK, HD), F32), unroll=4)
    inverse = lax.rsqrt(jnp.sum(squares, axis=1, keepdims=True) * (1.0 / D) + 1e-6)

    slot_ids = lax.broadcasted_iota(jnp.int32, (8 * CAP, TOK), 0)
    selector = jnp.where(slot_ids == srow_ref[...], 1.0, 0.0).astype(BF16)
    for n in range(4):
        cols = pl.ds(n * 512, 512)
        normed = (hid[:, cols] * inverse * gain_ref[:, cols]).astype(BF16)
        pk[:, cols] = jnp.dot(selector, normed, preferred_element_type=F32).astype(BF16)

    y_copies = []
    for j in (2, 1, 3):
        row = lax.rem(yh + j, 4)
        copy = remote(
            pk.at[rows_at(row * HALF, HALF), :], y.at[rows_at(yh * HALF, HALF), :],
            y_send.at[row], y_recv.at[yh], exp_dev(row, z),
        )
        copy.start()
        y_copies.append(copy)
    y[rows_at(yh * HALF, HALF), :] = pk[rows_at(yh * HALF, HALF), :]
    for j in (1, 3, 2):
        row = lax.rem(yh + j, 4)
        block = y.at[rows_at(row * HALF, HALF), :]
        pltpu.make_async_copy(block, block, y_recv.at[row]).wait()
    order = regroup(half, 0)
    for n in range(4):
        cols = pl.ds(n * 512, 512)
        sorted_rows = jnp.dot(order, y[:, cols], preferred_element_type=F32).astype(BF16)
        x[rows_at(z * ITEM, ITEM), cols] = sorted_rows[:ITEM]
        x[pl.ds(FAR * ITEM, ITEM), cols] = sorted_rows[ITEM:]

    def part(buffer, slot, j):
        return buffer.at[rows_at(slot * ITEM + j * HALF, HALF), :]

    far_dir_right = k >= 2
    far_dev = exp_dev(yh, jnp.where(far_dir_right, z_right, z_left))
    far_slot = jnp.where((k == 1) | (k == 2), PASS, z)
    far_copies = []
    for j in (0, 1):
        copy = remote(part(x, FAR, j), part(x, far_slot, j), f_send.at[j], x_recv.at[far_slot, j], far_dev)
        copy.start()
        far_copies.append(copy)

    has_right, has_left = k < 3, k > 0

    def forward(slot, dst_slot, j, to_right):
        return remote(
            part(x, slot, j), part(x, dst_slot, j),
            x_send.at[slot, jnp.where(to_right, 1, 0), j], x_recv.at[dst_slot, j],
            exp_dev(yh, jnp.where(to_right, z_right, z_left)),
        )

    for to_right, has in ((True, has_right), (False, has_left)):
        @pl.when(has)
        def _():
            for j in (0, 1):
                forward(z, z, j, to_right).start()

    for copy in w_locals:
        copy.wait()
    for copy in w_copies:
        copy.wait_recv()

    def experts(slot):
        at = rows_at(slot * ITEM, ITEM)
        active = jnp.maximum(jnp.dot(x[at, :], w1[...], preferred_element_type=F32), 0.0).astype(BF16)
        for n in range(4):
            cols = pl.ds(n * 512, 512)
            r[at, cols] = jnp.dot(active, w2[:, cols], preferred_element_type=F32).astype(BF16)

    def to_parent(slot, from_left, distance, j):
        edge = jnp.where(from_left, k == 0, k == 3)
        inner = jnp.where(from_left & (distance == 1), 8, slot)
        dst_slot = jnp.where(edge, 8 + distance, inner)
        return remote(
            part(r, slot, j), part(c, dst_slot, j), r_send.at[slot, j], c_recv.at[dst_slot, j],
            exp_dev(yh, jnp.where(from_left, z_left, z_right)),
        )

    experts(z)

    def arrive(s, carry):
        distance = lax.div(s, 2) + 1
        from_left = lax.rem(s, 2) == 0
        origin = lax.rem(jnp.where(from_left, z + 8 - distance, z + distance), 8)
        valid = jnp.where(from_left, distance <= k + 2, distance <= 5 - k)
        child = jnp.where(from_left, has_right, has_left)

        @pl.when((s == 2) & ((k == 0) | (k == 3)))
        def _():
            source = lax.rem(jnp.where(k == 3, z + 7, z + 1), 8)
            for j in (0, 1):
                pltpu.make_async_copy(part(x, PASS, j), part(x, PASS, j), x_recv.at[PASS, j]).wait()
                remote(
                    part(x, PASS, j), part(x, source, j), p_send.at[j], x_recv.at[source, j], far_dev
                ).start()

        @pl.when(valid)
        def _():
            for j in (0, 1):
                pltpu.make_async_copy(part(x, origin, j), part(x, origin, j), x_recv.at[origin, j]).wait()

                @pl.when(child)
                def _():
                    forward(origin, origin, j, from_left).start()

            experts(origin)

            @pl.when(jnp.logical_not(child))
            def _():
                for j in (0, 1):
                    to_parent(origin, from_left, distance, j).start()

        return carry

    lax.fori_loop(0, 10, arrive, 0)

    def add_child(slot, child_slot, j):
        pltpu.make_async_copy(part(c, child_slot, j), part(c, child_slot, j), c_recv.at[child_slot, j]).wait()
        at = rows_at(slot * ITEM + j * HALF, HALF)
        other = rows_at(child_slot * ITEM + j * HALF, HALF)
        r[at, :] = (r[at, :].astype(F32) + c[other, :].astype(F32)).astype(BF16)

    def give_back(from_left):
        count = jnp.where(from_left, k + 2, 5 - k)

        def one(s, carry):
            distance = s + 1

            @pl.when(distance <= count)
            def _():
                origin = lax.rem(jnp.where(from_left, z + 8 - distance, z + distance), 8)
                for j in (0, 1):
                    add_child(origin, origin, j)
                    to_parent(origin, from_left, distance, j).start()

            return carry

        lax.fori_loop(0, 5, one, 0)

    @pl.when((k == 1) | (k == 2))
    def _():
        give_back(k == 2)

    give_back(k < 2)

    @pl.when((k == 0) | (k == 3))
    def _():
        for j in (0, 1):
            pltpu.make_async_copy(part(c, 10, j), part(c, 10, j), c_recv.at[10, j]).wait()
            remote(
                part(c, 10, j), part(c, 9, j), p_send.at[2 + j], c_recv.at[9, j],
                exp_dev(yh, jnp.where(k == 3, z_left, z_right)),
            ).start()

    for j in (0, 1):
        @pl.when(has_left)
        def _():
            add_child(z, z, j)

        @pl.when(has_right)
        def _():
            add_child(z, 8, j)
        pltpu.make_async_copy(part(c, 9, j), part(c, 9, j), c_recv.at[9, j]).wait()

    order = regroup(half, 1)
    for n in range(4):
        cols = pl.ds(n * 512, 512)
        y[:, cols] = (
            jnp.dot(order[:, :ITEM], r[rows_at(z * ITEM, ITEM), cols], preferred_element_type=F32)
            + jnp.dot(order[:, ITEM:], c[pl.ds(FAR * ITEM, ITEM), cols], preferred_element_type=F32)
        ).astype(BF16)
    back = []
    for j in (2, 1, 3):
        row = lax.rem(yh + j, 4)
        copy = remote(
            y.at[rows_at(row * HALF, HALF), :], res.at[rows_at(yh * HALF, HALF), :],
            yr_send.at[row], res_recv.at[yh], exp_dev(row, z),
        )
        copy.start()
        back.append(copy)
    res[rows_at(yh * HALF, HALF), :] = y[rows_at(yh * HALF, HALF), :]
    for j in (1, 3, 2):
        row = lax.rem(yh + j, 4)
        block = res.at[rows_at(row * HALF, HALF), :]
        pltpu.make_async_copy(block, block, res_recv.at[row]).wait()

    slot_ids = lax.broadcasted_iota(jnp.int32, (TOK, 8 * CAP), 1)
    chosen = jnp.where(slot_ids == scol_ref[...], 1.0, 0.0).astype(BF16)
    for n in range(4):
        cols = pl.ds(n * 512, 512)
        picked = jnp.dot(chosen, res[:, cols], preferred_element_type=F32)
        out_ref[:, cols] = (hid[:, cols] + gate_ref[...] * picked).astype(BF16)

    for copy in kv_copies:
        copy.wait_send()
    for n in (5, 6, 7, 8):
        block = kvb.at[0, kv_slot(p), :]
        pltpu.make_async_copy(block, block, kv_send.at[n]).wait()
    for copy in w_copies + y_copies + back:
        copy.wait_send()
    for copy in far_copies:
        copy.wait_send()

    @pl.when((k == 0) | (k == 3))
    def _():
        for j in range(4):
            pltpu.make_async_copy(part(x, PASS, 0), part(x, PASS, 0), p_send.at[j]).wait()

    for to_right, has in ((True, has_right), (False, has_left)):
        @pl.when(has)
        def _():
            for j in (0, 1):
                forward(z, z, j, to_right).wait_send()

    def drain(s, carry):
        distance = lax.div(s, 2) + 1
        from_left = lax.rem(s, 2) == 0
        origin = lax.rem(jnp.where(from_left, z + 8 - distance, z + distance), 8)
        valid = jnp.where(from_left, distance <= k + 2, distance <= 5 - k)
        child = jnp.where(from_left, has_right, has_left)

        @pl.when(valid)
        def _():
            for j in (0, 1):
                @pl.when(child)
                def _():
                    forward(origin, origin, j, from_left).wait_send()
                to_parent(origin, from_left, distance, j).wait_send()

        return carry

    lax.fori_loop(0, 10, drain, 0)


def body(state, query, enc_kv, gain, w_in, w_out, expert_id, slot, gate):
    flat_slot = jnp.where(slot[0, 0] >= 0, expert_id[0, 0] * CAP + slot[0, 0], -1)
    vmem = pl.BlockSpec(memory_space=pltpu.VMEM)
    hbm = pl.BlockSpec(memory_space=pl.ANY)
    dma = pltpu.SemaphoreType.DMA
    out = pl.pallas_call(
        kernel,
        out_shape=jax.ShapeDtypeStruct((TOK, D), BF16),
        in_specs=[vmem] * 7 + [hbm] * 2,
        out_specs=vmem,
        scratch_shapes=[
            pltpu.VMEM((2, 8 * POS, D), BF16),
            pltpu.VMEM((TOK, D), F32),
            pltpu.VMEM((8 * CAP, D), BF16),
            pltpu.VMEM((8 * CAP, D), BF16),
            pltpu.VMEM((10 * ITEM, D), BF16),
            pltpu.VMEM((8 * ITEM, D), BF16),
            pltpu.VMEM((11 * ITEM, D), BF16),
            pltpu.VMEM((8 * CAP, D), BF16),
            pltpu.VMEM((D, 2 * FF), BF16),
            pltpu.VMEM((2 * FF, D), BF16),
            dma((9,)), dma((9,)), dma((2,)), dma((2,)), dma((2,)),
            dma((4,)), dma((4,)), dma((2,)), dma((9, 2)), dma((8, 2, 2)), dma((8, 2)), dma((11, 2)),
            dma((4,)), dma((4,)), dma((4,)),
        ],
        compiler_params=pltpu.CompilerParams(
            collective_id=0, has_side_effects=True, vmem_limit_bytes=50 * 1024 * 1024
        ),
        name="layer",
    )(
        state[0, 0], query[0, 0], jnp.transpose(enc_kv[0], (1, 0, 2)), gain.reshape(1, D),
        flat_slot.reshape(1, TOK), flat_slot.reshape(TOK, 1), gate[0, 0].reshape(TOK, 1), w_in, w_out,
    )
    return out.reshape(1, 1, TOK, D)


def solution(mesh):
    return jax.shard_map(
        body,
        mesh=mesh,
        in_specs=(
            P("expert", "pipe", None, None),
            P("expert", "pipe", None, None),
            P("expert", "pipe", None, None),
            P(),
            P(None, "expert"),
            P("expert", None),
            P("expert", "pipe", None),
            P("expert", "pipe", None),
            P("expert", "pipe", None),
        ),
        out_specs=P("expert", "pipe", None, None),
        check_vma=False,
    )
```

time: 510 us -> 191 us (0.37)
  the two profiles are of different devices: /device:TPU:288 before, /device:TPU:112 now
where the time goes in v1:
time: 191 us
  Pallas kernels  183 us (96%)
  local copies, waits for them, and re-layouts  6.88 us (4%)
    pallas_call x1, Pallas kernels, body(): pl.pallas_call(kernel, out_shape=jax.ShapeDtypeStruct((TOK, D), BF16), in...  183 us
    unnamed x10, local copies, waits for them, and re-layouts  6.01 us

profile of v1, /device:TPU:112, one launch (start us, length us, event | category | flops | bytes accessed | tf_op | source)
XLA Modules:
  0.0 190.9 jit_solution(12773579299041366715)
XLA Ops:
  0.0 0.7 fusion
  0.7 0.7 fusion.1.srow_ref
  1.4 0.1 copy.11.scol_ref
  1.5 0.8 copy.12.gate_ref
  2.2 1.0 copy.14
  3.3 0.0 copy-start
  3.3 1.4 copy-done
  4.7 0.0 copy-start.1
  4.7 1.0 copy-done.1
  5.7 0.0 copy-start.2
  5.7 1.0 copy-done.2
  6.8 0.0 copy-start.3
  6.8 0.7 copy-done.3
  7.5 182.6 %layer.1 = bf16[128,2048]{1,0:T(8,128)(2,1)S(1)} custom-call(bf16[128,2048]{1,0:T(8,128)(2,1)S(1)} %bitcast.16, bf16[128,2048]{1,0:T(8,128)(2,1)S(1)} %bitcast.17, bf16[2,32,2048]{2,1,0:T(8,128)(2,1)S(1)} %bitcast.15, f32[1,2048]{1,0:T(1,128)S(1)} %bitcast.18, s32[1,128]{1,0:T(1,128)S(1)} %fusion.1.srow_ref, s32[128,1]{1,0:T(8,128)S(1)} %copy.11.scol_ref, ...), custom_call_target="tpu_custom_call" | custom-call | tf_op jit(solution)/shard_map/layer/pallas_call | solution.py:378
  190.1 0.8 copy.16
Async XLA Ops:
  3.3 1.4 copy-start
  4.7 1.0 copy-start.1
  5.7 1.0 copy-start.2
  6.8 0.7 copy-start.3

commit v2 on v0

v2 whole, which is shorter than its diff:
```python
import math

import jax
import jax.numpy as jnp
from jax import lax
from jax.experimental import pallas as pl
from jax.experimental.pallas import tpu as pltpu
from jax.sharding import PartitionSpec as P

HEADS = 16
HD = 128
D = 2048
TOK = 128
CAP = 24
POS = 32
ITEM = 4 * CAP
PAIR = 2 * CAP
FF = 384
CHUNKS = 4
CW = D // CHUNKS
HW = CW // 2
PASS = 8
FAR = 9
MESH = pl.DeviceIdType.MESH
F32 = jnp.float32
BF16 = jnp.bfloat16

EDGE = (103549057, 153770258, 158000426, 162227756, 173811936, 2)
INNER = (103550097, 122063161, 124176818, 187633203, 173467866, 236464604)


def rows_at(start, count):
    return pl.ds(pl.multiple_of(start, 16), count)


def cols_at(n, width=CW):
    return pl.ds(pl.multiple_of(n * width, 128), width)


def one_hot(rows, cols, wanted, along):
    return jnp.where(lax.broadcasted_iota(jnp.int32, (rows, cols), along) == wanted, 1.0, 0.0).astype(BF16)


def split_order(half):
    at = lax.broadcasted_iota(jnp.int32, (2 * ITEM, 2 * ITEM), 0)
    far = (at >= ITEM).astype(jnp.int32)
    within = at - far * ITEM
    source = sum((within >= CAP * j).astype(jnp.int32) for j in (1, 2, 3))
    upper = far + half - 2 * far * half
    return one_hot(2 * ITEM, 2 * ITEM, within + source * CAP + upper * CAP, 1)


def home_order(side):
    at = lax.broadcasted_iota(jnp.int32, (2 * ITEM, ITEM), 0)
    source = sum((at >= PAIR * j).astype(jnp.int32) for j in (1, 2, 3))
    within = at - source * PAIR
    right = (within >= CAP).astype(jnp.int32)
    wanted = jnp.where(right == side, source * CAP + within - right * CAP, -1)
    return one_hot(2 * ITEM, ITEM, wanted, 1)


def kernel(
    state_ref, query_ref, kv_ref, gain_ref, srow_ref, scol_ref, upper_ref, gate_ref, win_ref, wout_ref,
    out_ref,
    kvb, hid, pk, y, x, r, c, home, res, w1, w2,
    kv_send, kv_recv, w_local, w_send, w_recv,
    y_send, y_recv, f_send, x_recv, x_send, r_send, c_recv, p_send, home_send, res_recv,
):
    p = lax.axis_index("pipe")
    i = lax.axis_index("expert")
    px, py = lax.rem(p, 4), lax.div(p, 4)
    yh, z, core = lax.div(i, 16), lax.rem(lax.div(i, 2), 8), lax.rem(i, 2)
    half, k = lax.div(z, 4), lax.rem(z, 4)

    def pipe_dev(row, xx):
        return {"pipe": row * 4 + xx}

    def exp_dev(row, zz):
        return {"expert": (row * 8 + zz) * 2 + core}

    x_right, x_left = lax.rem(px + 1, 4), lax.rem(px + 3, 4)
    z_right, z_left = lax.rem(z + 1, 8), lax.rem(z + 7, 8)
    sibling = {"expert": i + 1 - 2 * core}

    w_locals = [
        pltpu.make_async_copy(win_ref, w1.at[:, pl.ds(0, FF)], w_local.at[0]),
        pltpu.make_async_copy(wout_ref, w2.at[pl.ds(0, FF), :], w_local.at[1]),
    ]
    for copy in w_locals:
        copy.start()

    barrier = pltpu.get_barrier_semaphore()
    peers = [
        pipe_dev(1 - py, px), pipe_dev(py, x_right), pipe_dev(py, x_left),
        sibling, exp_dev(yh, z_right), exp_dev(yh, z_left),
    ] + [exp_dev(lax.rem(yh + j, 4), z) for j in (1, 2, 3)]
    for peer in peers:
        pl.semaphore_signal(barrier, inc=1, device_id=peer, device_id_type=MESH)
    pl.semaphore_wait(barrier, len(peers))

    def remote(src, dst, send, recv, device):
        return pltpu.make_async_remote_copy(
            src_ref=src, dst_ref=dst, send_sem=send, recv_sem=recv,
            device_id=device, device_id_type=MESH,
        )

    def arrived(block, sem):
        pltpu.make_async_copy(block, block, sem).wait()

    def kv_slot(owner):
        return pl.ds(pl.multiple_of(owner * POS, POS), POS)

    partner = (1 - py) * 4 + px
    routes = (pipe_dev(1 - py, px), pipe_dev(py, x_right), pipe_dev(py, x_left))

    def kv_own(n, way):
        return remote(
            kv_ref.at[:, :, cols_at(n)], kvb.at[:, kv_slot(p), cols_at(n)],
            kv_send.at[n, way], kv_recv.at[n, way], routes[way],
        )

    def kv_partner(n, way):
        block = kvb.at[:, kv_slot(partner), cols_at(n)]
        return remote(block, block, kv_send.at[n, 2 + way], kv_recv.at[n, 2 + way], routes[way])

    def kv_on(n, row, way):
        block = kvb.at[way - 1, kv_slot(row * 4 + (x_left if way == 1 else x_right)), cols_at(n)]
        at = 4 + way + (0 if row is py else 2)
        return remote(block, block, kv_send.at[n, at], kv_recv.at[n, at], routes[way])

    def kv_first(n):
        for way in (0, 1, 2):
            kv_own(n, way).start()

    def kv_second(n):
        kv_own(n, 0).wait_recv()
        for way in (1, 2):
            kv_partner(n, way).start()

    def kv_third(n):
        for way in (1, 2):
            kv_own(n, way).wait_recv()
            kv_on(n, py, way).start()
        for way in (1, 2):
            kv_partner(n, way).wait_recv()
            kv_on(n, 1 - py, way).start()

    def kv_last(n):
        for row in (py, 1 - py):
            for way in (1, 2):
                kv_on(n, row, way).wait_recv()

    scale = 1.0 / math.sqrt(HD)
    selector = one_hot(8 * CAP, TOK, srow_ref[...], 0)
    to_kinds = split_order(half)

    def attend(n, squares):
        for h in range(HEADS // CHUNKS):
            cols = pl.ds(pl.multiple_of(n * CW + h * HD, HD), HD)
            scores = lax.dot_general(
                query_ref[:, cols], kvb[0, :, cols], (((1,), (1,)), ((), ())), preferred_element_type=F32
            ) * scale
            raised = jnp.exp(scores - jnp.max(scores, axis=1, keepdims=True))
            denominator = jnp.sum(raised, axis=1, keepdims=True)
            mixed = jnp.dot(raised.astype(BF16), kvb[1, :, cols], preferred_element_type=F32)
            hidden = state_ref[:, cols].astype(F32) + mixed / denominator
            hid[:, cols] = hidden
            squares = squares + hidden * hidden
        return squares

    def y_copy(n, j):
        row = lax.rem(yh + j, 4)
        return remote(
            pk.at[rows_at(row * PAIR, PAIR), cols_at(n)], y.at[rows_at(yh * PAIR, PAIR), cols_at(n)],
            y_send.at[n, j], y_recv.at[n, j], exp_dev(row, z),
        )

    def pack(n):
        cols = cols_at(n)
        scaled = (hid[:, cols] * gain_ref[:, cols]).astype(BF16)
        pk[:, cols] = jnp.dot(selector, scaled, preferred_element_type=F32).astype(BF16)
        for j in (2, 1, 3):
            y_copy(n, j).start()
        y[rows_at(yh * PAIR, PAIR), cols] = pk[rows_at(yh * PAIR, PAIR), cols]

    def part(buffer, slot, n):
        return buffer.at[rows_at(slot * ITEM, ITEM), cols_at(n)]

    outer_right = k >= 2
    outer = exp_dev(yh, jnp.where(outer_right, z_right, z_left))
    far_slot = jnp.where((k == 1) | (k == 2), PASS, z)
    has_right, has_left = k < 3, k > 0

    def forward(slot, n, to_right):
        return remote(
            part(x, slot, n), part(x, slot, n),
            x_send.at[slot, jnp.where(to_right, 1, 0), n], x_recv.at[slot, n],
            exp_dev(yh, jnp.where(to_right, z_right, z_left)),
        )

    def far_copy(n):
        return remote(part(x, FAR, n), part(x, far_slot, n), f_send.at[n], x_recv.at[far_slot, n], outer)

    def spread(n):
        cols = cols_at(n)
        for j in (1, 3, 2):
            y_copy(n, j).wait_recv()
        sorted_rows = jnp.dot(to_kinds, y[:, cols], preferred_element_type=F32).astype(BF16)
        x[pl.ds(FAR * ITEM, ITEM), cols] = sorted_rows[ITEM:]
        x[rows_at(z * ITEM, ITEM), cols] = sorted_rows[:ITEM]
        far_copy(n).start()
        for to_right, has in ((True, has_right), (False, has_left)):
            @pl.when(has)
            def _():
                forward(z, n, to_right).start()

    for n in (0, 1):
        kv_first(n)
    w_copies = [
        remote(win_ref, w1.at[:, pl.ds(FF, FF)], w_send.at[0], w_recv.at[0], sibling),
        remote(wout_ref, w2.at[pl.ds(FF, FF), :], w_send.at[1], w_recv.at[1], sibling),
    ]
    for copy in w_copies:
        copy.start()
    kvb[:, kv_slot(p), :] = kv_ref[...]
    kv_second(0)
    kv_third(0)
    squares = jnp.zeros((TOK, HD), F32)
    for n in range(CHUNKS):
        if n + 2 < CHUNKS:
            kv_first(n + 2)
        if n + 1 < CHUNKS:
            kv_second(n + 1)
        kv_last(n)
        if n + 1 < CHUNKS:
            kv_third(n + 1)
        squares = attend(n, squares)
        pack(n)
        if n:
            spread(n - 1)
    inverse = lax.rsqrt(jnp.sum(squares, axis=1, keepdims=True) * (1.0 / D) + 1e-6)
    spread(CHUNKS - 1)
    for copy in w_locals:
        copy.wait()
    for copy in w_copies:
        copy.wait_recv()

    def experts(slot):
        at = rows_at(slot * ITEM, ITEM)
        active = jnp.maximum(jnp.dot(x[at, :], w1[...], preferred_element_type=F32), 0.0).astype(BF16)
        for n in range(CHUNKS):
            cols = cols_at(n)
            r[at, cols] = jnp.dot(active, w2[:, cols], preferred_element_type=F32).astype(BF16)

    def to_parent(slot, from_left, distance, n):
        edge = jnp.where(from_left, k == 0, k == 3)
        inner = jnp.where(from_left & (distance == 1), PASS, slot)
        dst_slot = jnp.where(edge, PASS + distance, inner)
        return remote(
            part(r, slot, n), part(c, dst_slot, n), r_send.at[slot, n], c_recv.at[dst_slot, n],
            exp_dev(yh, jnp.where(from_left, z_left, z_right)),
        )

    def pass_block(n):
        source = lax.rem(jnp.where(outer_right, z + 7, z + 1), 8)
        return remote(part(x, PASS, n), part(x, source, n), p_send.at[0, n], x_recv.at[source, n], outer)

    def pass_result(n):
        inward = exp_dev(yh, jnp.where(outer_right, z_left, z_right))
        return remote(part(c, 10, n), part(c, FAR, n), p_send.at[1, n], c_recv.at[FAR, n], inward)

    def home_copy(kind, n, j):
        row = lax.rem(yh + j, 4)
        return remote(
            home.at[kind, rows_at(row * PAIR, PAIR), cols_at(n, HW)],
            res.at[kind, rows_at(yh * PAIR, PAIR), cols_at(n, HW)],
            home_send.at[kind, n, j], res_recv.at[kind, n, j], exp_dev(row, z),
        )

    left_half, right_half = home_order(0), home_order(1)

    def send_home(kind, n, rows):
        cols = cols_at(n, HW)
        home[kind, :, cols] = (
            jnp.dot(left_half, rows[:, :HW], preferred_element_type=F32)
            + jnp.dot(right_half, rows[:, HW:], preferred_element_type=F32)
        ).astype(BF16)
        for j in (2, 1, 3):
            home_copy(kind, n, j).start()
        res[kind, rows_at(yh * PAIR, PAIR), cols] = home[kind, rows_at(yh * PAIR, PAIR), cols]

    words = [jnp.where((k == 0) | (k == 3), a, b) for a, b in zip(EDGE, INNER)]

    def step(t, carry):
        word = words[0]
        for n in range(1, len(words)):
            word = jnp.where(lax.div(t, 4) == n, words[n], word)
        at = lax.rem(t, 4)
        code = jnp.where(
            at == 0, lax.rem(word, 128),
            jnp.where(
                at == 1, lax.rem(lax.div(word, 128), 128),
                jnp.where(at == 2, lax.rem(lax.div(word, 16384), 128), lax.div(word, 2097152)),
            ),
        )
        op, side, distance = lax.div(code, 16), lax.rem(lax.div(code, 8), 2), lax.rem(code, 8)
        from_left = (side == 0) != outer_right
        origin = lax.rem(jnp.where(from_left, z + 8 - distance, z + distance), 8)

        @pl.when((op == 0) & (distance == 1))
        def _():
            def one(n, carry):
                arrived(part(x, PASS, n), x_recv.at[PASS, n])
                pass_block(n).start()
                return carry
            lax.fori_loop(0, CHUNKS, one, 0)

        @pl.when((op == 0) & (distance == 2))
        def _():
            def one(n, carry):
                arrived(part(c, 10, n), c_recv.at[10, n])
                pass_result(n).start()
                return carry
            lax.fori_loop(0, CHUNKS, one, 0)

        @pl.when(op == 1)
        def _():
            def one(n, carry):
                arrived(part(x, origin, n), x_recv.at[origin, n])
                forward(origin, n, from_left).start()
                return carry
            lax.fori_loop(0, CHUNKS, one, 0)

        @pl.when(op == 2)
        def _():
            def one(n, carry):
                arrived(part(x, origin, n), x_recv.at[origin, n])
                return carry
            lax.fori_loop(0, CHUNKS, one, 0)

        @pl.when((op == 2) | (op == 3))
        def _():
            experts(origin)

        @pl.when((op == 4) | (op == 5))
        def _():
            def one(n, carry):
                @pl.when(op == 5)
                def _():
                    arrived(part(c, origin, n), c_recv.at[origin, n])
                    at = rows_at(origin * ITEM, ITEM)
                    cols = cols_at(n)
                    r[at, cols] = (r[at, cols].astype(F32) + c[at, cols].astype(F32)).astype(BF16)
                to_parent(origin, from_left, distance, n).start()
                return carry
            lax.fori_loop(0, CHUNKS, one, 0)

        @pl.when(op == 6)
        def _():
            def one(n, carry):
                at = rows_at(z * ITEM, ITEM)
                cols = cols_at(n)
                for slot, has in ((z, has_left), (PASS, has_right)):
                    @pl.when(has)
                    def _():
                        arrived(part(c, slot, n), c_recv.at[slot, n])
                        other = rows_at(slot * ITEM, ITEM)
                        r[at, cols] = (r[at, cols].astype(F32) + c[other, cols].astype(F32)).astype(BF16)
                send_home(0, n, r[at, cols])
                return carry
            lax.fori_loop(0, CHUNKS, one, 0)

        @pl.when(op == 7)
        def _():
            def one(n, carry):
                arrived(part(c, FAR, n), c_recv.at[FAR, n])
                send_home(1, n, c[pl.ds(FAR * ITEM, ITEM), cols_at(n)])
                return carry
            lax.fori_loop(0, CHUNKS, one, 0)

        return carry

    lax.fori_loop(0, 4 * len(words), step, 0)

    near = upper_ref[...] == half
    weight = gate_ref[...] * inverse
    chosen = []
    for kind in (0, 1):
        base = jnp.where(near == (kind == 0), scol_ref[...], -PAIR)
        chosen.append([one_hot(TOK, 2 * ITEM, base + side * CAP, 1) for side in (0, 1)])
    for n in range(CHUNKS):
        for kind in (0, 1):
            for j in (1, 3, 2):
                home_copy(kind, n, j).wait_recv()
        for side in (0, 1):
            cols = pl.ds(n * CW + side * HW, HW)
            picked = sum(
                jnp.dot(chosen[kind][side], res[kind, :, pl.ds(n * HW, HW)], preferred_element_type=F32)
                for kind in (0, 1)
            )
            out_ref[:, cols] = (hid[:, cols] + weight * picked).astype(BF16)

    for copy in w_copies:
        copy.wait_send()

    def drain(n, carry):
        for way in (0, 1, 2):
            kv_own(n, way).wait_send()
        for way in (1, 2):
            kv_partner(n, way).wait_send()
            for row in (py, 1 - py):
                kv_on(n, row, way).wait_send()
        for j in (1, 2, 3):
            y_copy(n, j).wait_send()
            for kind in (0, 1):
                home_copy(kind, n, j).wait_send()
        far_copy(n).wait_send()
        for to_right, has in ((True, has_right), (False, has_left)):
            @pl.when(has)
            def _():
                forward(z, n, to_right).wait_send()

        @pl.when((k == 0) | (k == 3))
        def _():
            pass_block(n).wait_send()
            pass_result(n).wait_send()

        def one(s, carry):
            distance = lax.div(s, 2) + 1
            from_left = lax.rem(s, 2) == 0
            origin = lax.rem(jnp.where(from_left, z + 8 - distance, z + distance), 8)

            @pl.when(jnp.where(from_left, distance <= k + 2, distance <= 5 - k))
            def _():
                @pl.when(jnp.where(from_left, has_right, has_left))
                def _():
                    forward(origin, n, from_left).wait_send()
                to_parent(origin, from_left, distance, n).wait_send()
            return carry

        return lax.fori_loop(0, 10, one, carry)

    lax.fori_loop(0, CHUNKS, drain, 0)


def body(state, query, enc_kv, gain, w_in, w_out, expert_id, slot, gate):
    expert, place = expert_id[0, 0], slot[0, 0]
    kept = place >= 0
    flat_slot = jnp.where(kept, expert * CAP + place, -1)
    home_row = jnp.where(kept, (expert // 2) * PAIR + place, -PAIR)
    vmem = pl.BlockSpec(memory_space=pltpu.VMEM)
    hbm = pl.BlockSpec(memory_space=pl.ANY)
    dma = pltpu.SemaphoreType.DMA
    out = pl.pallas_call(
        kernel,
        out_shape=jax.ShapeDtypeStruct((TOK, D), BF16),
        in_specs=[vmem] * 8 + [hbm] * 2,
        out_specs=vmem,
        scratch_shapes=[
            pltpu.VMEM((2, 8 * POS, D), BF16),
            pltpu.VMEM((TOK, D), F32),
            pltpu.VMEM((8 * CAP, D), BF16),
            pltpu.VMEM((8 * CAP, D), BF16),
            pltpu.VMEM((10 * ITEM, D), BF16),
            pltpu.VMEM((8 * ITEM, D), BF16),
            pltpu.VMEM((11 * ITEM, D), BF16),
            pltpu.VMEM((2, 2 * ITEM, D // 2), BF16),
            pltpu.VMEM((2, 2 * ITEM, D // 2), BF16),
            pltpu.VMEM((D, 2 * FF), BF16),
            pltpu.VMEM((2 * FF, D), BF16),
            dma((4, 9)), dma((4, 9)), dma((2,)), dma((2,)), dma((2,)),
            dma((4, 4)), dma((4, 4)), dma((4,)), dma((9, 4)), dma((8, 2, 4)), dma((8, 4)), dma((11, 4)),
            dma((2, 4)), dma((2, 4, 4)), dma((2, 4, 4)),
        ],
        compiler_params=pltpu.CompilerParams(
            collective_id=0, has_side_effects=True, vmem_limit_bytes=50 * 1024 * 1024
        ),
        name="layer",
    )(
        state[0, 0], query[0, 0], jnp.transpose(enc_kv[0], (1, 0, 2)), gain.reshape(1, D),
        flat_slot.reshape(1, TOK), home_row.reshape(TOK, 1), (expert % 2).reshape(TOK, 1),
        gate[0, 0].reshape(TOK, 1), w_in, w_out,
    )
    return out.reshape(1, 1, TOK, D)


def solution(mesh):
    return jax.shard_map(
        body,
        mesh=mesh,
        in_specs=(
            P("expert", "pipe", None, None),
            P("expert", "pipe", None, None),
            P("expert", "pipe", None, None),
            P(),
            P(None, "expert"),
            P("expert", None),
            P("expert", "pipe", None),
            P("expert", "pipe", None),
            P("expert", "pipe", None),
        ),
        out_specs=P("expert", "pipe", None, None),
        check_vma=False,
    )
```

time: 510 us -> 151 us (0.30)
  the two profiles are of different devices: /device:TPU:288 before, /device:TPU:72 now
where the time goes in v2:
time: 151 us; the launch traced here: 150 us
  Pallas kernels  141 us (93%)
  local copies, waits for them, and re-layouts  8.29 us (5%)
    pallas_call x1, Pallas kernels, body(): pl.pallas_call(kernel, out_shape=jax.ShapeDtypeStruct((TOK, D), BF16), in...  141 us
    unnamed x10, local copies, waits for them, and re-layouts  6.01 us

profile of v2, /device:TPU:72, one launch (start us, length us, event | category | flops | bytes accessed | tf_op | source)
XLA Modules:
  0.0 150.3 jit_solution(8455665757217808550)
XLA Ops:
  0.0 0.7 fusion.5.srow_ref
  0.7 0.8 copy.17.gate_ref
  1.4 0.8 copy.11
  2.2 0.8 copy.12
  3.0 0.1 add_select_fusion
  3.0 1.0 copy.19
  4.1 0.0 copy-start
  4.1 1.4 copy-done
  5.5 0.0 copy-start.1
  5.5 1.0 copy-done.1
  6.5 0.0 copy-start.2
  6.5 1.0 copy-done.2
  7.6 0.0 copy-start.3
  7.6 0.7 copy-done.3
  8.3 141.3 %layer.1 = bf16[128,2048]{1,0:T(8,128)(2,1)S(1)} custom-call(bf16[128,2048]{1,0:T(8,128)(2,1)S(1)} %bitcast.16, bf16[128,2048]{1,0:T(8,128)(2,1)S(1)} %bitcast.17, bf16[2,32,2048]{2,1,0:T(8,128)(2,1)S(1)} %bitcast.15, f32[1,2048]{1,0:T(1,128)S(1)} %bitcast.18, s32[1,128]{1,0:T(1,128)S(1)} %fusion.5.srow_ref, s32[128,1]{1,0:T(8,128)S(1)} %get-tuple-element.6.scol_ref, ...), custom_call_target="tpu_custom_call" | custom-call | tf_op jit(solution)/shard_map/layer/pallas_call | solution.py:454
  149.5 0.8 copy.21
Async XLA Ops:
  4.1 1.4 copy-start
  5.5 1.0 copy-start.1
  6.5 1.0 copy-start.2
  7.6 0.7 copy-start.3

commit v3 on v2

--- a/solution.py
+++ b/solution.py
@@ -25,8 +25,9 @@
 F32 = jnp.float32
 BF16 = jnp.bfloat16
 
-EDGE = (103549057, 153770258, 158000426, 162227756, 173811936, 2)
-INNER = (103550097, 122063161, 124176818, 187633203, 173467866, 236464604)
+EDGE = (88375441, 91395249, 106108491, 170665645, 201369929, 112)
+INNER = (54824081, 57580720, 59558331, 103587418, 175581531, 236465361)
+WEIGHTS = 3
 
 
 def rows_at(start, count):
@@ -60,10 +61,10 @@
 
 
 def kernel(
-    state_ref, query_ref, kv_ref, gain_ref, srow_ref, scol_ref, upper_ref, gate_ref, win_ref, wout_ref,
+    kv_ref, state_hbm, query_hbm, gain_hbm, expert_hbm, slot_hbm, gate_hbm, win_ref, wout_ref,
     out_ref,
-    kvb, hid, pk, y, x, r, c, home, res, w1, w2,
-    kv_send, kv_recv, w_local, w_send, w_recv,
+    state_ref, query_ref, gain_ref, expert_ref, slot_ref, gate_ref, kvb, hid, pk, y, x, r, c, home, res, w1, w2,
+    present, in_sem, kv_send, kv_recv, w_local, w_send, w_recv,
     y_send, y_recv, f_send, x_recv, x_send, r_send, c_recv, p_send, home_send, res_recv,
 ):
     p = lax.axis_index("pipe")
@@ -82,6 +83,15 @@
     z_right, z_left = lax.rem(z + 1, 8), lax.rem(z + 7, 8)
     sibling = {"expert": i + 1 - 2 * core}
 
+    inputs = [
+        pltpu.make_async_copy(src, dst, in_sem.at[n])
+        for n, (src, dst) in enumerate((
+            (expert_hbm, expert_ref), (slot_hbm, slot_ref), (gate_hbm, gate_ref), (gain_hbm, gain_ref),
+            (query_hbm, query_ref), (state_hbm, state_ref),
+        ))
+    ]
+    for copy in inputs:
+        copy.start()
     w_locals = [
         pltpu.make_async_copy(win_ref, w1.at[:, pl.ds(0, FF)], w_local.at[0]),
         pltpu.make_async_copy(wout_ref, w2.at[pl.ds(0, FF), :], w_local.at[1]),
@@ -92,11 +102,21 @@
     barrier = pltpu.get_barrier_semaphore()
     peers = [
         pipe_dev(1 - py, px), pipe_dev(py, x_right), pipe_dev(py, x_left),
-        sibling, exp_dev(yh, z_right), exp_dev(yh, z_left),
+        exp_dev(yh, z_right), exp_dev(yh, z_left),
     ] + [exp_dev(lax.rem(yh + j, 4), z) for j in (1, 2, 3)]
     for peer in peers:
         pl.semaphore_signal(barrier, inc=1, device_id=peer, device_id_type=MESH)
-    pl.semaphore_wait(barrier, len(peers))
+
+    @pl.when(core == 0)
+    def _():
+        pl.semaphore_signal(barrier, inc=1, device_id=sibling, device_id_type=MESH)
+        pl.semaphore_wait(barrier, len(peers))
+
+    @pl.when(core == 1)
+    def _():
+        pl.semaphore_wait(barrier, len(peers) + 1)
+        pl.semaphore_signal(present, inc=1, device_id=sibling, device_id_type=MESH)
+
 
     def remote(src, dst, send, recv, device):
         return pltpu.make_async_remote_copy(
@@ -107,62 +127,68 @@
     def arrived(block, sem):
         pltpu.make_async_copy(block, block, sem).wait()
 
+    w_copies = [
+        remote(win_ref, w1.at[:, pl.ds(FF, FF)], w_send.at[0], w_recv.at[0], sibling),
+        remote(wout_ref, w2.at[pl.ds(FF, FF), :], w_send.at[1], w_recv.at[1], sibling),
+    ]
+
+    @pl.when(core == 1)
+    def _():
+        for copy in w_copies:
+            copy.start()
+
     def kv_slot(owner):
         return pl.ds(pl.multiple_of(owner * POS, POS), POS)
 
-    partner = (1 - py) * 4 + px
     routes = (pipe_dev(1 - py, px), pipe_dev(py, x_right), pipe_dev(py, x_left))
 
-    def kv_own(n, way):
+    def kv_pair(column):
+        return pl.ds(pl.multiple_of(column * 2 * POS, 2 * POS), 2 * POS)
+
+    def kv_own(n):
         return remote(
-            kv_ref.at[:, :, cols_at(n)], kvb.at[:, kv_slot(p), cols_at(n)],
-            kv_send.at[n, way], kv_recv.at[n, way], routes[way],
-        )
-
-    def kv_partner(n, way):
-        block = kvb.at[:, kv_slot(partner), cols_at(n)]
+            kv_ref.at[:, :, cols_at(n)], kvb.at[n, :, kv_slot(px * 2 + py), :],
+            kv_send.at[n, 0], kv_recv.at[n, 0], routes[0],
+        )
+
+    def kv_both(n, way):
+        block = kvb.at[n, :, kv_pair(px), :]
+        return remote(block, block, kv_send.at[n, way], kv_recv.at[n, way], routes[way])
+
+    def kv_on(n, way):
+        block = kvb.at[n, way - 1, kv_pair(x_left if way == 1 else x_right), :]
         return remote(block, block, kv_send.at[n, 2 + way], kv_recv.at[n, 2 + way], routes[way])
 
-    def kv_on(n, row, way):
-        block = kvb.at[way - 1, kv_slot(row * 4 + (x_left if way == 1 else x_right)), cols_at(n)]
-        at = 4 + way + (0 if row is py else 2)
-        return remote(block, block, kv_send.at[n, at], kv_recv.at[n, at], routes[way])
-
     def kv_first(n):
-        for way in (0, 1, 2):
-            kv_own(n, way).start()
+        kv_own(n).start()
 
     def kv_second(n):
-        kv_own(n, 0).wait_recv()
+        kv_own(n).wait_recv()
         for way in (1, 2):
-            kv_partner(n, way).start()
+            kv_both(n, way).start()
 
     def kv_third(n):
         for way in (1, 2):
-            kv_own(n, way).wait_recv()
-            kv_on(n, py, way).start()
+            kv_both(n, way).wait_recv()
+            kv_on(n, way).start()
+
+    def kv_last(n):
         for way in (1, 2):
-            kv_partner(n, way).wait_recv()
-            kv_on(n, 1 - py, way).start()
-
-    def kv_last(n):
-        for row in (py, 1 - py):
-            for way in (1, 2):
-                kv_on(n, row, way).wait_recv()
+            kv_on(n, way).wait_recv()
 
     scale = 1.0 / math.sqrt(HD)
-    selector = one_hot(8 * CAP, TOK, srow_ref[...], 0)
     to_kinds = split_order(half)
 
     def attend(n, squares):
         for h in range(HEADS // CHUNKS):
             cols = pl.ds(pl.multiple_of(n * CW + h * HD, HD), HD)
+            inside = pl.ds(h * HD, HD)
             scores = lax.dot_general(
-                query_ref[:, cols], kvb[0, :, cols], (((1,), (1,)), ((), ())), preferred_element_type=F32
+                query_ref[:, cols], kvb[n, 0, :, inside], (((1,), (1,)), ((), ())), preferred_element_type=F32
             ) * scale
             raised = jnp.exp(scores - jnp.max(scores, axis=1, keepdims=True))
             denominator = jnp.sum(raised, axis=1, keepdims=True)
-            mixed = jnp.dot(raised.astype(BF16), kvb[1, :, cols], preferred_element_type=F32)
+            mixed = jnp.dot(raised.astype(BF16), kvb[n, 1, :, inside], preferred_element_type=F32)
             hidden = state_ref[:, cols].astype(F32) + mixed / denominator
             hid[:, cols] = hidden
             squares = squares + hidden * hidden
@@ -171,20 +197,20 @@
     def y_copy(n, j):
         row = lax.rem(yh + j, 4)
         return remote(
-            pk.at[rows_at(row * PAIR, PAIR), cols_at(n)], y.at[rows_at(yh * PAIR, PAIR), cols_at(n)],
+            pk.at[n, rows_at(row * PAIR, PAIR), :], y.at[n, rows_at(yh * PAIR, PAIR), :],
             y_send.at[n, j], y_recv.at[n, j], exp_dev(row, z),
         )
 
     def pack(n):
         cols = cols_at(n)
         scaled = (hid[:, cols] * gain_ref[:, cols]).astype(BF16)
-        pk[:, cols] = jnp.dot(selector, scaled, preferred_element_type=F32).astype(BF16)
+        pk[n] = jnp.dot(selector, scaled, preferred_element_type=F32).astype(BF16)
         for j in (2, 1, 3):
             y_copy(n, j).start()
-        y[rows_at(yh * PAIR, PAIR), cols] = pk[rows_at(yh * PAIR, PAIR), cols]
+        y[n, rows_at(yh * PAIR, PAIR), :] = pk[n, rows_at(yh * PAIR, PAIR), :]
 
     def part(buffer, slot, n):
-        return buffer.at[rows_at(slot * ITEM, ITEM), cols_at(n)]
+        return buffer.at[n, rows_at(slot * ITEM, ITEM), :]
 
     outer_right = k >= 2
     outer = exp_dev(yh, jnp.where(outer_right, z_right, z_left))
@@ -202,55 +228,59 @@
         return remote(part(x, FAR, n), part(x, far_slot, n), f_send.at[n], x_recv.at[far_slot, n], outer)
 
     def spread(n):
-        cols = cols_at(n)
         for j in (1, 3, 2):
             y_copy(n, j).wait_recv()
-        sorted_rows = jnp.dot(to_kinds, y[:, cols], preferred_element_type=F32).astype(BF16)
-        x[pl.ds(FAR * ITEM, ITEM), cols] = sorted_rows[ITEM:]
-        x[rows_at(z * ITEM, ITEM), cols] = sorted_rows[:ITEM]
+        sorted_rows = jnp.dot(to_kinds, y[n], preferred_element_type=F32).astype(BF16)
+        x[n, pl.ds(FAR * ITEM, ITEM), :] = sorted_rows[ITEM:]
+        x[n, rows_at(z * ITEM, ITEM), :] = sorted_rows[:ITEM]
         far_copy(n).start()
         for to_right, has in ((True, has_right), (False, has_left)):
             @pl.when(has)
             def _():
                 forward(z, n, to_right).start()
 
-    for n in (0, 1):
+    for n in range(CHUNKS):
         kv_first(n)
-    w_copies = [
-        remote(win_ref, w1.at[:, pl.ds(FF, FF)], w_send.at[0], w_recv.at[0], sibling),
-        remote(wout_ref, w2.at[pl.ds(FF, FF), :], w_send.at[1], w_recv.at[1], sibling),
-    ]
-    for copy in w_copies:
-        copy.start()
-    kvb[:, kv_slot(p), :] = kv_ref[...]
+    for n in range(CHUNKS):
+        kvb[n, :, kv_slot(px * 2 + py), :] = kv_ref[:, :, pl.ds(n * CW, CW)]
     kv_second(0)
+    kv_second(1)
     kv_third(0)
+    for copy in inputs:
+        copy.wait()
+    expert, place = expert_ref[...], slot_ref[...]
+    kept = place >= 0
+    selector = one_hot(8 * CAP, TOK, jnp.where(kept, expert * CAP + place, -1), 0)
     squares = jnp.zeros((TOK, HD), F32)
     for n in range(CHUNKS):
         if n + 2 < CHUNKS:
-            kv_first(n + 2)
-        if n + 1 < CHUNKS:
-            kv_second(n + 1)
-        kv_last(n)
+            kv_second(n + 2)
         if n + 1 < CHUNKS:
             kv_third(n + 1)
+        kv_last(n)
         squares = attend(n, squares)
         pack(n)
+        if n == 1:
+            @pl.when(core == 0)
+            def _():
+                pl.semaphore_wait(present, 1)
+                for copy in w_copies:
+                    copy.start()
+
         if n:
             spread(n - 1)
     inverse = lax.rsqrt(jnp.sum(squares, axis=1, keepdims=True) * (1.0 / D) + 1e-6)
     spread(CHUNKS - 1)
-    for copy in w_locals:
-        copy.wait()
-    for copy in w_copies:
-        copy.wait_recv()
 
     def experts(slot):
         at = rows_at(slot * ITEM, ITEM)
-        active = jnp.maximum(jnp.dot(x[at, :], w1[...], preferred_element_type=F32), 0.0).astype(BF16)
+        total = sum(
+            jnp.dot(x[n, at, :], w1[pl.ds(n * CW, CW), :], preferred_element_type=F32) for n in range(CHUNKS)
+        )
+        active = jnp.maximum(total, 0.0).astype(BF16)
         for n in range(CHUNKS):
-            cols = cols_at(n)
-            r[at, cols] = jnp.dot(active, w2[:, cols], preferred_element_type=F32).astype(BF16)
+            cols = pl.ds(n * CW, CW)
+            r[n, at, :] = jnp.dot(active, w2[:, cols], preferred_element_type=F32).astype(BF16)
 
     def to_parent(slot, from_left, distance, n):
         edge = jnp.where(from_left, k == 0, k == 3)
@@ -272,22 +302,21 @@
     def home_copy(kind, n, j):
         row = lax.rem(yh + j, 4)
         return remote(
-            home.at[kind, rows_at(row * PAIR, PAIR), cols_at(n, HW)],
-            res.at[kind, rows_at(yh * PAIR, PAIR), cols_at(n, HW)],
+            home.at[kind, n, rows_at(row * PAIR, PAIR), :],
+            res.at[kind, n, rows_at(yh * PAIR, PAIR), :],
             home_send.at[kind, n, j], res_recv.at[kind, n, j], exp_dev(row, z),
         )
 
     left_half, right_half = home_order(0), home_order(1)
 
     def send_home(kind, n, rows):
-        cols = cols_at(n, HW)
-        home[kind, :, cols] = (
+        home[kind, n] = (
             jnp.dot(left_half, rows[:, :HW], preferred_element_type=F32)
             + jnp.dot(right_half, rows[:, HW:], preferred_element_type=F32)
         ).astype(BF16)
         for j in (2, 1, 3):
             home_copy(kind, n, j).start()
-        res[kind, rows_at(yh * PAIR, PAIR), cols] = home[kind, rows_at(yh * PAIR, PAIR), cols]
+        res[kind, n, rows_at(yh * PAIR, PAIR), :] = home[kind, n, rows_at(yh * PAIR, PAIR), :]
 
     words = [jnp.where((k == 0) | (k == 3), a, b) for a, b in zip(EDGE, INNER)]
 
@@ -307,6 +336,13 @@
         from_left = (side == 0) != outer_right
         origin = lax.rem(jnp.where(from_left, z + 8 - distance, z + distance), 8)
 
+        @pl.when(t == WEIGHTS)
+        def _():
+            for copy in w_locals:
+                copy.wait()
+            for copy in w_copies:
+                copy.wait_recv()
+
         @pl.when((op == 0) & (distance == 1))
         def _():
             def one(n, carry):
@@ -349,8 +385,7 @@
                 def _():
                     arrived(part(c, origin, n), c_recv.at[origin, n])
                     at = rows_at(origin * ITEM, ITEM)
-                    cols = cols_at(n)
-                    r[at, cols] = (r[at, cols].astype(F32) + c[at, cols].astype(F32)).astype(BF16)
+                    r[n, at, :] = (r[n, at, :].astype(F32) + c[n, at, :].astype(F32)).astype(BF16)
                 to_parent(origin, from_left, distance, n).start()
                 return carry
             lax.fori_loop(0, CHUNKS, one, 0)
@@ -359,14 +394,13 @@
         def _():
             def one(n, carry):
                 at = rows_at(z * ITEM, ITEM)
-                cols = cols_at(n)
                 for slot, has in ((z, has_left), (PASS, has_right)):
                     @pl.when(has)
                     def _():
                         arrived(part(c, slot, n), c_recv.at[slot, n])
                         other = rows_at(slot * ITEM, ITEM)
-                        r[at, cols] = (r[at, cols].astype(F32) + c[other, cols].astype(F32)).astype(BF16)
-                send_home(0, n, r[at, cols])
+                        r[n, at, :] = (r[n, at, :].astype(F32) + c[n, other, :].astype(F32)).astype(BF16)
+                send_home(0, n, r[n, at, :])
                 return carry
             lax.fori_loop(0, CHUNKS, one, 0)
 
@@ -374,7 +408,7 @@
         def _():
             def one(n, carry):
                 arrived(part(c, FAR, n), c_recv.at[FAR, n])
-                send_home(1, n, c[pl.ds(FAR * ITEM, ITEM), cols_at(n)])
+                send_home(1, n, c[n, pl.ds(FAR * ITEM, ITEM), :])
                 return carry
             lax.fori_loop(0, CHUNKS, one, 0)
 
@@ -382,11 +416,17 @@
 
     lax.fori_loop(0, 4 * len(words), step, 0)
 
-    near = upper_ref[...] == half
-    weight = gate_ref[...] * inverse
+    def column(row):
+        same = lax.broadcasted_iota(jnp.int32, (TOK, TOK), 0) == lax.broadcasted_iota(jnp.int32, (TOK, TOK), 1)
+        return jnp.sum(jnp.where(same, row, 0.0), axis=1, keepdims=True)
+
+    pair = lax.shift_right_logical(expert, 1)
+    home_row = column(jnp.where(kept, pair * PAIR + place, -PAIR).astype(F32)).astype(jnp.int32)
+    near = column((expert - 2 * pair == half).astype(F32))
+    weight = column(gate_ref[...]) * inverse
     chosen = []
     for kind in (0, 1):
-        base = jnp.where(near == (kind == 0), scol_ref[...], -PAIR)
+        base = jnp.where(near == 1.0 - kind, home_row, -PAIR)
         chosen.append([one_hot(TOK, 2 * ITEM, base + side * CAP, 1) for side in (0, 1)])
     for n in range(CHUNKS):
         for kind in (0, 1):
@@ -395,7 +435,7 @@
         for side in (0, 1):
             cols = pl.ds(n * CW + side * HW, HW)
             picked = sum(
-                jnp.dot(chosen[kind][side], res[kind, :, pl.ds(n * HW, HW)], preferred_element_type=F32)
+                jnp.dot(chosen[kind][side], res[kind, n], preferred_element_type=F32)
                 for kind in (0, 1)
             )
             out_ref[:, cols] = (hid[:, cols] + weight * picked).astype(BF16)
@@ -404,12 +444,10 @@
         copy.wait_send()
 
     def drain(n, carry):
-        for way in (0, 1, 2):
-            kv_own(n, way).wait_send()
+        kv_own(n).wait_send()
         for way in (1, 2):
-            kv_partner(n, way).wait_send()
-            for row in (py, 1 - py):
-                kv_on(n, row, way).wait_send()
+            kv_both(n, way).wait_send()
+            kv_on(n, way).wait_send()
         for j in (1, 2, 3):
             y_copy(n, j).wait_send()
             for kind in (0, 1):
@@ -444,42 +482,43 @@
 
 
 def body(state, query, enc_kv, gain, w_in, w_out, expert_id, slot, gate):
-    expert, place = expert_id[0, 0], slot[0, 0]
-    kept = place >= 0
-    flat_slot = jnp.where(kept, expert * CAP + place, -1)
-    home_row = jnp.where(kept, (expert // 2) * PAIR + place, -PAIR)
     vmem = pl.BlockSpec(memory_space=pltpu.VMEM)
-    hbm = pl.BlockSpec(memory_space=pl.ANY)
+    hbm = pl.BlockSpec(memory_space=pltpu.HBM)
     dma = pltpu.SemaphoreType.DMA
     out = pl.pallas_call(
         kernel,
         out_shape=jax.ShapeDtypeStruct((TOK, D), BF16),
-        in_specs=[vmem] * 8 + [hbm] * 2,
+        in_specs=[vmem] + [hbm] * 8,
         out_specs=vmem,
         scratch_shapes=[
-            pltpu.VMEM((2, 8 * POS, D), BF16),
+            pltpu.VMEM((TOK, D), BF16),
+            pltpu.VMEM((TOK, D), BF16),
+            pltpu.VMEM((1, D), F32),
+            pltpu.VMEM((1, TOK), jnp.int32),
+            pltpu.VMEM((1, TOK), jnp.int32),
+            pltpu.VMEM((1, TOK), F32),
+            pltpu.VMEM((CHUNKS, 2, 8 * POS, CW), BF16),
             pltpu.VMEM((TOK, D), F32),
-            pltpu.VMEM((8 * CAP, D), BF16),
-            pltpu.VMEM((8 * CAP, D), BF16),
-            pltpu.VMEM((10 * ITEM, D), BF16),
-            pltpu.VMEM((8 * ITEM, D), BF16),
-            pltpu.VMEM((11 * ITEM, D), BF16),
-            pltpu.VMEM((2, 2 * ITEM, D // 2), BF16),
-            pltpu.VMEM((2, 2 * ITEM, D // 2), BF16),
+            pltpu.VMEM((CHUNKS, 8 * CAP, CW), BF16),
+            pltpu.VMEM((CHUNKS, 8 * CAP, CW), BF16),
+            pltpu.VMEM((CHUNKS, 10 * ITEM, CW), BF16),
+            pltpu.VMEM((CHUNKS, 8 * ITEM, CW), BF16),
+            pltpu.VMEM((CHUNKS, 11 * ITEM, CW), BF16),
+            pltpu.VMEM((2, CHUNKS, 2 * ITEM, HW), BF16),
+            pltpu.VMEM((2, CHUNKS, 2 * ITEM, HW), BF16),
             pltpu.VMEM((D, 2 * FF), BF16),
             pltpu.VMEM((2 * FF, D), BF16),
-            dma((4, 9)), dma((4, 9)), dma((2,)), dma((2,)), dma((2,)),
-            dma((4, 4)), dma((4, 4)), dma((4,)), dma((9, 4)), dma((8, 2, 4)), dma((8, 4)), dma((11, 4)),
-            dma((2, 4)), dma((2, 4, 4)), dma((2, 4, 4)),
+            pltpu.SemaphoreType.REGULAR, dma((6,)), dma((CHUNKS, 5)), dma((CHUNKS, 5)), dma((2,)), dma((2,)), dma((2,)),
+            dma((CHUNKS, 4)), dma((CHUNKS, 4)), dma((CHUNKS,)), dma((9, CHUNKS)), dma((8, 2, CHUNKS)),
+            dma((8, CHUNKS)), dma((11, CHUNKS)), dma((2, CHUNKS)), dma((2, CHUNKS, 4)), dma((2, CHUNKS, 4)),
         ],
         compiler_params=pltpu.CompilerParams(
-            collective_id=0, has_side_effects=True, vmem_limit_bytes=50 * 1024 * 1024
+            collective_id=0, has_side_effects=True, vmem_limit_bytes=60 * 1024 * 1024
         ),
         name="layer",
     )(
-        state[0, 0], query[0, 0], jnp.transpose(enc_kv[0], (1, 0, 2)), gain.reshape(1, D),
-        flat_slot.reshape(1, TOK), home_row.reshape(TOK, 1), (expert % 2).reshape(TOK, 1),
-        gate[0, 0].reshape(TOK, 1), w_in, w_out,
+        jnp.transpose(enc_kv[0], (1, 0, 2)), state[0, 0], query[0, 0], gain.reshape(1, D),
+        expert_id[0], slot[0], gate[0], w_in, w_out,
     )
     return out.reshape(1, 1, TOK, D)
 

time: 151 us -> 141 us (0.934)
  the two profiles are of different devices: /device:TPU:72 before, /device:TPU:8 now
where the time goes in v3:
time: 141 us
  Pallas kernels  138 us (98%)
  local copies, waits for them, and re-layouts  3.61 us (3%)
    pallas_call x1, Pallas kernels, body(): pl.pallas_call(kernel, out_shape=jax.ShapeDtypeStruct((TOK, D), BF16), in...  138 us
    unnamed x2, local copies, waits for them, and re-layouts  3.61 us

profile of v3, /device:TPU:8, one launch (start us, length us, event | category | flops | bytes accessed | tf_op | source)
XLA Modules:
  0.0 141.2 jit_solution(13121212736805563853)
XLA Ops:
  0.0 1.7 %copy.12 = bf16[1,32,2,2048]{3,1,2,0:T(8,128)(2,1)} copy(bf16[1,32,2,2048]{3,2,1,0:T(2,128)(2,1)} %param.11) | data formatting | bytes 524288 | tf_op args[2]
  1.7 137.6 %layer.1 = bf16[128,2048]{1,0:T(8,128)(2,1)} custom-call(bf16[2,32,2048]{2,1,0:T(8,128)(2,1)} %bitcast.13, bf16[128,2048]{1,0:T(8,128)(2,1)} %bitcast.14, bf16[128,2048]{1,0:T(8,128)(2,1)} %bitcast.15, f32[1,2048]{1,0:T(1,128)} %bitcast.16, s32[1,128]{1,0:T(1,128)} %bitcast.17, s32[1,128]{1,0:T(1,128)} %bitcast.18, f32[1,128]{1,0:T(1,128)} %bitcast.19, ...), custom_call_target="tpu_custom_call" | custom-call | tf_op jit(solution)/shard_map/layer/pallas_call | solution.py:488
  139.3 1.9 %copy.14 = bf16[1,1,128,2048]{3,2,1,0:T(8,128)(2,1)} copy(bf16[1,1,128,2048]{3,2,1,0:T(8,128)(2,1)} %bitcast.12) | data formatting | bytes 1048576

commit v4 on v3

--- a/solution.py
+++ b/solution.py
@@ -79,6 +79,9 @@
     def exp_dev(row, zz):
         return {"expert": (row * 8 + zz) * 2 + core}
 
+    def y_dev(row, plane):
+        return {"pipe": plane * 4 + px, "expert": (lax.rem(row, 4) * 8 + z) * 2 + core}
+
     x_right, x_left = lax.rem(px + 1, 4), lax.rem(px + 3, 4)
     z_right, z_left = lax.rem(z + 1, 8), lax.rem(z + 7, 8)
     sibling = {"expert": i + 1 - 2 * core}
@@ -103,7 +106,8 @@
     peers = [
         pipe_dev(1 - py, px), pipe_dev(py, x_right), pipe_dev(py, x_left),
         exp_dev(yh, z_right), exp_dev(yh, z_left),
-    ] + [exp_dev(lax.rem(yh + j, 4), z) for j in (1, 2, 3)]
+        y_dev(yh + 1, 0), y_dev(yh + 3, 1), y_dev(yh + 2, 1 - py), y_dev(jnp.where(py == 0, yh + 3, yh + 1), py),
+    ]
     for peer in peers:
         pl.semaphore_signal(barrier, inc=1, device_id=peer, device_id_type=MESH)
 
@@ -194,20 +198,22 @@
             squares = squares + hidden * hidden
         return squares
 
-    def y_copy(n, j):
-        row = lax.rem(yh + j, 4)
+    def y_copy(n, way):
+        row = lax.rem(yh + (1, 3, 2)[way], 4)
+        plane = (0, 1, 1 - py)[way]
+        place = 3 if way == 2 else 1 + py
         return remote(
-            pk.at[n, rows_at(row * PAIR, PAIR), :], y.at[n, rows_at(yh * PAIR, PAIR), :],
-            y_send.at[n, j], y_recv.at[n, j], exp_dev(row, z),
+            pk.at[n, rows_at(row * PAIR, PAIR), :], y.at[n, rows_at(place * PAIR, PAIR), :],
+            y_send.at[n, way], y_recv.at[n, place], y_dev(row, plane),
         )
 
     def pack(n):
         cols = cols_at(n)
         scaled = (hid[:, cols] * gain_ref[:, cols]).astype(BF16)
         pk[n] = jnp.dot(selector, scaled, preferred_element_type=F32).astype(BF16)
-        for j in (2, 1, 3):
-            y_copy(n, j).start()
-        y[n, rows_at(yh * PAIR, PAIR), :] = pk[n, rows_at(yh * PAIR, PAIR), :]
+        for way in (2, 0, 1):
+            y_copy(n, way).start()
+        y[n, pl.ds(0, PAIR), :] = pk[n, rows_at(yh * PAIR, PAIR), :]
 
     def part(buffer, slot, n):
         return buffer.at[n, rows_at(slot * ITEM, ITEM), :]
@@ -228,8 +234,8 @@
         return remote(part(x, FAR, n), part(x, far_slot, n), f_send.at[n], x_recv.at[far_slot, n], outer)
 
     def spread(n):
-        for j in (1, 3, 2):
-            y_copy(n, j).wait_recv()
+        for place in (1, 2, 3):
+            arrived(y.at[n, pl.ds(place * PAIR, PAIR), :], y_recv.at[n, place])
         sorted_rows = jnp.dot(to_kinds, y[n], preferred_element_type=F32).astype(BF16)
         x[n, pl.ds(FAR * ITEM, ITEM), :] = sorted_rows[ITEM:]
         x[n, rows_at(z * ITEM, ITEM), :] = sorted_rows[:ITEM]
@@ -260,7 +266,7 @@
         kv_last(n)
         squares = attend(n, squares)
         pack(n)
-        if n == 1:
+        if n == 2:
             @pl.when(core == 0)
             def _():
                 pl.semaphore_wait(present, 1)
@@ -299,12 +305,13 @@
         inward = exp_dev(yh, jnp.where(outer_right, z_left, z_right))
         return remote(part(c, 10, n), part(c, FAR, n), p_send.at[1, n], c_recv.at[FAR, n], inward)
 
-    def home_copy(kind, n, j):
-        row = lax.rem(yh + j, 4)
+    def home_copy(kind, n, place):
+        row = yh + 2 if place == 3 else jnp.where(py == 0, yh + 3, yh + 1)
+        plane = 1 - py if place == 3 else place - 1
+        way = 2 if place == 3 else py
         return remote(
-            home.at[kind, n, rows_at(row * PAIR, PAIR), :],
-            res.at[kind, n, rows_at(yh * PAIR, PAIR), :],
-            home_send.at[kind, n, j], res_recv.at[kind, n, j], exp_dev(row, z),
+            home.at[kind, n, pl.ds(place * PAIR, PAIR), :], res.at[kind, n, rows_at(yh * PAIR, PAIR), :],
+            home_send.at[kind, n, place], res_recv.at[kind, n, way], y_dev(row, plane),
         )
 
     left_half, right_half = home_order(0), home_order(1)
@@ -314,9 +321,9 @@
             jnp.dot(left_half, rows[:, :HW], preferred_element_type=F32)
             + jnp.dot(right_half, rows[:, HW:], preferred_element_type=F32)
         ).astype(BF16)
-        for j in (2, 1, 3):
-            home_copy(kind, n, j).start()
-        res[kind, n, rows_at(yh * PAIR, PAIR), :] = home[kind, n, rows_at(yh * PAIR, PAIR), :]
+        for place in (3, 1, 2):
+            home_copy(kind, n, place).start()
+        res[kind, n, rows_at(yh * PAIR, PAIR), :] = home[kind, n, pl.ds(0, PAIR), :]
 
     words = [jnp.where((k == 0) | (k == 3), a, b) for a, b in zip(EDGE, INNER)]
 
@@ -416,6 +423,44 @@
 
     lax.fori_loop(0, 4 * len(words), step, 0)
 
+    for copy in w_copies:
+        copy.wait_send()
+
+    def drain(n, carry):
+        kv_own(n).wait_send()
+        for way in (1, 2):
+            kv_both(n, way).wait_send()
+            kv_on(n, way).wait_send()
+        for way in (0, 1, 2):
+            y_copy(n, way).wait_send()
+        far_copy(n).wait_send()
+        for to_right, has in ((True, has_right), (False, has_left)):
+            @pl.when(has)
+            def _():
+                forward(z, n, to_right).wait_send()
+
+        @pl.when((k == 0) | (k == 3))
+        def _():
+            pass_block(n).wait_send()
+            pass_result(n).wait_send()
+
+        def one(s, carry):
+            distance = lax.div(s, 2) + 1
+            from_left = lax.rem(s, 2) == 0
+            origin = lax.rem(jnp.where(from_left, z + 8 - distance, z + distance), 8)
+
+            @pl.when(jnp.where(from_left, distance <= k + 2, distance <= 5 - k))
+            def _():
+                @pl.when(jnp.where(from_left, has_right, has_left))
+                def _():
+                    forward(origin, n, from_left).wait_send()
+                to_parent(origin, from_left, distance, n).wait_send()
+            return carry
+
+        return lax.fori_loop(0, 10, one, carry)
+
+    lax.fori_loop(0, CHUNKS, drain, 0)
+
     def column(row):
         same = lax.broadcasted_iota(jnp.int32, (TOK, TOK), 0) == lax.broadcasted_iota(jnp.int32, (TOK, TOK), 1)
         return jnp.sum(jnp.where(same, row, 0.0), axis=1, keepdims=True)
@@ -430,8 +475,8 @@
         chosen.append([one_hot(TOK, 2 * ITEM, base + side * CAP, 1) for side in (0, 1)])
     for n in range(CHUNKS):
         for kind in (0, 1):
-            for j in (1, 3, 2):
-                home_copy(kind, n, j).wait_recv()
+            for way in (0, 1, 2):
+                arrived(res.at[kind, n, pl.ds(0, PAIR), :], res_recv.at[kind, n, way])
         for side in (0, 1):
             cols = pl.ds(n * CW + side * HW, HW)
             picked = sum(
@@ -439,46 +484,10 @@
                 for kind in (0, 1)
             )
             out_ref[:, cols] = (hid[:, cols] + weight * picked).astype(BF16)
-
-    for copy in w_copies:
-        copy.wait_send()
-
-    def drain(n, carry):
-        kv_own(n).wait_send()
-        for way in (1, 2):
-            kv_both(n, way).wait_send()
-            kv_on(n, way).wait_send()
-        for j in (1, 2, 3):
-            y_copy(n, j).wait_send()
-            for kind in (0, 1):
-                home_copy(kind, n, j).wait_send()
-        far_copy(n).wait_send()
-        for to_right, has in ((True, has_right), (False, has_left)):
-            @pl.when(has)
-            def _():
-                forward(z, n, to_right).wait_send()
-
-        @pl.when((k == 0) | (k == 3))
-        def _():
-            pass_block(n).wait_send()
-            pass_result(n).wait_send()
-
-        def one(s, carry):
-            distance = lax.div(s, 2) + 1
-            from_left = lax.rem(s, 2) == 0
-            origin = lax.rem(jnp.where(from_left, z + 8 - distance, z + distance), 8)
-
-            @pl.when(jnp.where(from_left, distance <= k + 2, distance <= 5 - k))
-            def _():
-                @pl.when(jnp.where(from_left, has_right, has_left))
-                def _():
-                    forward(origin, n, from_left).wait_send()
-                to_parent(origin, from_left, distance, n).wait_send()
-            return carry
-
-        return lax.fori_loop(0, 10, one, carry)
-
-    lax.fori_loop(0, CHUNKS, drain, 0)
+    for n in range(CHUNKS):
+        for kind in (0, 1):
+            for place in (1, 2, 3):
+                home_copy(kind, n, place).wait_send()
 
 
 def body(state, query, enc_kv, gain, w_in, w_out, expert_id, slot, gate):

time: 141 us -> 139 us (0.986)
  Pallas kernels: 138 us -> 135 us
    pallas_call x1, Pallas kernels: 138 us -> 135 us  [body(): pl.pallas_call(kernel, out_shape=jax.ShapeDtypeStruct((TOK, D), BF16), in...]
where the time goes in v4:
time: 139 us
  Pallas kernels  135 us (97%)
  local copies, waits for them, and re-layouts  3.61 us (3%)
    pallas_call x1, Pallas kernels, body(): pl.pallas_call(kernel, out_shape=jax.ShapeDtypeStruct((TOK, D), BF16), in...  135 us
    unnamed x2, local copies, waits for them, and re-layouts  3.61 us

profile of v4, /device:TPU:8, one launch (start us, length us, event | category | flops | bytes accessed | tf_op | source)
XLA Modules:
  0.0 139.1 jit_solution(7321712155492431296)
XLA Ops:
  0.0 1.7 %copy.12 = bf16[1,32,2,2048]{3,1,2,0:T(8,128)(2,1)} copy(bf16[1,32,2,2048]{3,2,1,0:T(2,128)(2,1)} %param.11) | data formatting | bytes 524288 | tf_op args[2]
  1.7 135.4 %layer.1 = bf16[128,2048]{1,0:T(8,128)(2,1)} custom-call(bf16[2,32,2048]{2,1,0:T(8,128)(2,1)} %bitcast.13, bf16[128,2048]{1,0:T(8,128)(2,1)} %bitcast.14, bf16[128,2048]{1,0:T(8,128)(2,1)} %bitcast.15, f32[1,2048]{1,0:T(1,128)} %bitcast.16, s32[1,128]{1,0:T(1,128)} %bitcast.17, s32[1,128]{1,0:T(1,128)} %bitcast.18, f32[1,128]{1,0:T(1,128)} %bitcast.19, ...), custom_call_target="tpu_custom_call" | custom-call | tf_op jit(solution)/shard_map/layer/pallas_call | solution.py:497
  137.2 1.9 %copy.14 = bf16[1,1,128,2048]{3,2,1,0:T(8,128)(2,1)} copy(bf16[1,1,128,2048]{3,2,1,0:T(8,128)(2,1)} %bitcast.12) | data formatting | bytes 1048576

commit v5 on v4

--- a/solution.py
+++ b/solution.py
@@ -25,8 +25,8 @@
 F32 = jnp.float32
 BF16 = jnp.bfloat16
 
-EDGE = (88375441, 91395249, 106108491, 170665645, 201369929, 112)
-INNER = (54824081, 57580720, 59558331, 103587418, 175581531, 236465361)
+EDGE = (90474625, 157964593, 162227756, 171074858, 4991344, 96)
+INNER = (103058705, 122603931, 127323292, 194288050, 102034745, 236464345)
 WEIGHTS = 3
 
 

time: 139 us -> 130 us (0.935)
  Pallas kernels: 135 us -> 126 us
    pallas_call x1, Pallas kernels: 135 us -> 126 us  [body(): pl.pallas_call(kernel, out_shape=jax.ShapeDtypeStruct((TOK, D), BF16), in...]
where the time goes in v5:
time: 130 us
  Pallas kernels  126 us (97%)
  local copies, waits for them, and re-layouts  3.61 us (3%)
    pallas_call x1, Pallas kernels, body(): pl.pallas_call(kernel, out_shape=jax.ShapeDtypeStruct((TOK, D), BF16), in...  126 us
    unnamed x2, local copies, waits for them, and re-layouts  3.61 us

profile of v5, /device:TPU:8, one launch (start us, length us, event | category | flops | bytes accessed | tf_op | source)
XLA Modules:
  0.0 129.7 jit_solution(15733462596068562702)
XLA Ops:
  0.0 1.7 %copy.12 = bf16[1,32,2,2048]{3,1,2,0:T(8,128)(2,1)} copy(bf16[1,32,2,2048]{3,2,1,0:T(2,128)(2,1)} %param.11) | data formatting | bytes 524288 | tf_op args[2]
  1.7 126.1 %layer.1 = bf16[128,2048]{1,0:T(8,128)(2,1)} custom-call(bf16[2,32,2048]{2,1,0:T(8,128)(2,1)} %bitcast.13, bf16[128,2048]{1,0:T(8,128)(2,1)} %bitcast.14, bf16[128,2048]{1,0:T(8,128)(2,1)} %bitcast.15, f32[1,2048]{1,0:T(1,128)} %bitcast.16, s32[1,128]{1,0:T(1,128)} %bitcast.17, s32[1,128]{1,0:T(1,128)} %bitcast.18, f32[1,128]{1,0:T(1,128)} %bitcast.19, ...), custom_call_target="tpu_custom_call" | custom-call | tf_op jit(solution)/shard_map/layer/pallas_call | solution.py:497
  127.8 1.9 %copy.14 = bf16[1,1,128,2048]{3,2,1,0:T(8,128)(2,1)} copy(bf16[1,1,128,2048]{3,2,1,0:T(8,128)(2,1)} %bitcast.12) | data formatting | bytes 1048576

commit v6 on v5

--- a/solution.py
+++ b/solution.py
@@ -252,6 +252,7 @@
     kv_second(0)
     kv_second(1)
     kv_third(0)
+    kv_second(2)
     for copy in inputs:
         copy.wait()
     expert, place = expert_ref[...], slot_ref[...]
@@ -259,13 +260,13 @@
     selector = one_hot(8 * CAP, TOK, jnp.where(kept, expert * CAP + place, -1), 0)
     squares = jnp.zeros((TOK, HD), F32)
     for n in range(CHUNKS):
-        if n + 2 < CHUNKS:
-            kv_second(n + 2)
         if n + 1 < CHUNKS:
             kv_third(n + 1)
         kv_last(n)
         squares = attend(n, squares)
         pack(n)
+        if n + 3 < CHUNKS:
+            kv_second(n + 3)
         if n == 2:
             @pl.when(core == 0)
             def _():

time: 130 us -> 130 us (level)
  no operation moved by 1% of the time
where the time goes in v6:
time: 130 us
  Pallas kernels  126 us (97%)
  local copies, waits for them, and re-layouts  3.61 us (3%)
    pallas_call x1, Pallas kernels, body(): pl.pallas_call(kernel, out_shape=jax.ShapeDtypeStruct((TOK, D), BF16), in...  126 us
    unnamed x2, local copies, waits for them, and re-layouts  3.61 us

profile of v6, /device:TPU:8, one launch (start us, length us, event | category | flops | bytes accessed | tf_op | source)
XLA Modules:
  0.0 129.7 jit_solution(83947466542701010)
XLA Ops:
  0.0 1.7 %copy.12 = bf16[1,32,2,2048]{3,1,2,0:T(8,128)(2,1)} copy(bf16[1,32,2,2048]{3,2,1,0:T(2,128)(2,1)} %param.11) | data formatting | bytes 524288 | tf_op args[2]
  1.7 126.1 %layer.1 = bf16[128,2048]{1,0:T(8,128)(2,1)} custom-call(bf16[2,32,2048]{2,1,0:T(8,128)(2,1)} %bitcast.13, bf16[128,2048]{1,0:T(8,128)(2,1)} %bitcast.14, bf16[128,2048]{1,0:T(8,128)(2,1)} %bitcast.15, f32[1,2048]{1,0:T(1,128)} %bitcast.16, s32[1,128]{1,0:T(1,128)} %bitcast.17, s32[1,128]{1,0:T(1,128)} %bitcast.18, f32[1,128]{1,0:T(1,128)} %bitcast.19, ...), custom_call_target="tpu_custom_call" | custom-call | tf_op jit(solution)/shard_map/layer/pallas_call | solution.py:498
  127.8 1.9 %copy.14 = bf16[1,1,128,2048]{3,2,1,0:T(8,128)(2,1)} copy(bf16[1,1,128,2048]{3,2,1,0:T(8,128)(2,1)} %bitcast.12) | data formatting | bytes 1048576
